TPU v7x, 256 devices: a whole 4x4x8 slice. The times are simulated.
256 devices in a mesh: section: 2 (over core), dp: 8 (over y, z_lo), tensor: 16 (over x, z_hi).
Axes of the slice: x: 4, y: 4, z: 8 (z_hi: 4, z_lo: 2; z = z_hi * 2 + z_lo), core: 2. Of those that a mesh axis runs over, the one named last changes fastest.
Arguments:
- residual_parts: bfloat16 [2, 3072, 16384], P('section', 'dp', 'tensor'), may hold values from -120 to 120
- attn_out: bfloat16 [2, 3072, 16384], P('section', 'dp', 'tensor'), may hold values from -6 to 6
- ffn_input: bfloat16 [2, 3072, 53248], P('section', 'dp', 'tensor'), may hold values from -6 to 6
- norm_gain: float32 [2, 16384], P('section', 'tensor'), may hold values from 0.25 to 1.75
- mixing: bfloat16 [2, 52, 52], P('section'), may hold values from -0.875 to 0.875
- blocks: int32 [2, 2], P('section'), may hold values from 0 to 25, as said below
Outputs:
- hess_in: float32 [2, 16384, 1024], P('section', 'tensor', 'dp')
- hess_o: float32 [2, 16384, 1024], P('section', 'tensor', 'dp')
- hess_down: float32 [2, 2048, 2048], P('section', 'tensor', 'dp')
Inputs may be any that keep to these rules, and one draw needn't show every extreme that they name: `blocks`: entry [s, 0] is below 16; entry [s, 1] is below 26. In every draw one layer has entry [s, 0] = 0 and entry [s, 1] = 25.
All inputs are finite; a program needn't handle non-finite values.
Results may differ from a plain program's by a relative error of at most 0.0038.
Values may be sent and summed in bfloat16 or wider, within the bound.
No kernel may reach another device: no remote copies, remote signals or barrier semaphores. Data moves between devices by JAX's collectives and lax.ppermute only.
A program may use at most 64 MiB of HBM per device.

v0:
```python
import math
import jax
import jax.numpy as jnp
from jax import lax
from jax.sharding import Mesh
from jax.sharding import PartitionSpec as P

D = 16384
KB = 52
HBLK = 1024
BLK = 2048
TENSOR = ("tensor_0", "tensor_1")
EPS = 1e-05


def passed_along(x, axis, by):
    devices = lax.axis_size(axis)
    pairs = [(i, i + by) for i in range(devices) if 0 <= i + by < devices]
    return lax.ppermute(x, axis, pairs)


def copy_for_each(x, axis):
    devices = lax.axis_size(axis)
    return lax.all_to_all(jnp.broadcast_to(x[None], (devices, *x.shape)), axis, 0, 0, tiled=True)


def over_copies(x, axis):
    everything = copy_for_each(x, axis)
    return jnp.sum(everything, axis=0)


def broadcast_by_axis(x, axes, root):
    x = jnp.where(lax.axis_index(axes) == root, x, jnp.zeros_like(x))
    for axis in axes:
        x = lax.psum(x, axis)
    return x


def in_blocks(x, dim, devices):
    before, after = (x.shape[:dim], x.shape[dim + 1 :])
    return jnp.moveaxis(x.reshape(*before, devices, -1, *after), dim, 0)


def summed_on_arrival(x, axis, dim):
    tiles = in_blocks(x, dim, lax.axis_size(axis))
    arrived = lax.all_to_all(tiles, axis, split_axis=0, concat_axis=0, tiled=True)
    return arrived.sum(axis=0)


def in_one_piece(arrays, axis, dim, along):
    both = jnp.concatenate(arrays, axis=along)
    out, at, done = (lax.psum_scatter(both, axis, scatter_dimension=dim, tiled=True), 0, [])
    for a in arrays:
        done.append(lax.slice_in_dim(out, at, at + a.shape[along], axis=along))
        at += a.shape[along]
    return tuple(done)


def bit_parity(values):
    total = jnp.zeros_like(values)
    for position in range(16):
        total = total + values // (1 << position) % 2
    return total % 2


def sylvester(order):
    index = jnp.arange(order, dtype=jnp.int32)
    parity = bit_parity(jnp.bitwise_and(index[:, None], index[None, :]))
    return (1 - 2 * parity).astype(jnp.float32)


def gram(left, right):
    return lax.dot_general(
        left, right, (((0,), (0,)), ((), ())), preferred_element_type=jnp.float32
    )


def local(residual_parts, attn_out, ffn_input, norm_gain, mixing, blocks):
    local_d = residual_parts.shape[2]
    local_f = ffn_input.shape[2]
    token_rows = residual_parts.shape[1]
    own_part = residual_parts[0]
    earlier = passed_along(own_part, "section", 1)
    layer_in = earlier.astype(jnp.float32) + own_part.astype(jnp.float32)
    square_total = over_copies(jnp.sum(layer_in * layer_in, axis=1), TENSOR)
    normed = (layer_in * lax.rsqrt(square_total / D + EPS)[:, None] * norm_gain[0][None, :]).astype(
        jnp.bfloat16
    )
    attention = attn_out[0]
    first_col = blocks[0, 0] * HBLK
    norm_list, attn_list = ([], [])
    owner = first_col // local_d + 0
    norm_got = broadcast_by_axis(normed, TENSOR, owner)
    attn_got = broadcast_by_axis(attention, TENSOR, owner)
    norm_list.append(norm_got)
    attn_list.append(attn_got)
    norm_block = norm_list[0]
    attn_block = attn_list[0]
    tensor_count = lax.axis_size(TENSOR)
    member = lax.axis_index(TENSOR)
    a_local = local_f // KB
    order_a = a_local * tensor_count
    cube = ffn_input[0].reshape(token_rows, a_local, KB)
    mixed = jnp.einsum("rak,kc->rac", cube, mixing[0], preferred_element_type=jnp.float32)
    turned = jnp.einsum("rac,ae->rec", mixed, sylvester(a_local), precision=lax.Precision.HIGHEST)
    turned = turned.reshape(token_rows, local_f)
    start = blocks[0, 1] * BLK
    doubled = jnp.concatenate([turned, turned], axis=1)
    window = lax.dynamic_slice_in_dim(doubled, start % local_f, BLK, 1)
    target = (start + jnp.arange(BLK, dtype=jnp.int32)) // local_f
    parity = bit_parity(jnp.bitwise_and(target, member))
    signs = (1 - 2 * parity).astype(jnp.float32) / math.sqrt(order_a)
    term = window * signs[None, :]
    own_cols = summed_on_arrival(term, TENSOR, 1).astype(jnp.bfloat16)
    rotated = lax.all_gather(own_cols, TENSOR, axis=1, tiled=True)
    part_in = gram(normed, norm_block)
    part_o = gram(attention, attn_block)
    part_down = gram(own_cols, rotated)
    summed = (
        *in_one_piece((part_in, part_o), "dp", 1, 0),
        lax.psum_scatter(part_down, "dp", scatter_dimension=1, tiled=True),
    )
    scale = 2.0 / (token_rows * lax.axis_size("dp"))
    hess_in = (scale * summed[0])[None]
    hess_o = (scale * summed[1])[None]
    hess_down = (scale * summed[2])[None]
    return (hess_in, hess_o, hess_down)


def solution(mesh):
    finer = Mesh(
        mesh.devices.reshape(mesh.shape["section"], mesh.shape["dp"], 4, 4),
        ("section", "dp", "tensor_0", "tensor_1"),
    )
    in_specs = (
        P("section", "dp", TENSOR),
        P("section", "dp", TENSOR),
        P("section", "dp", TENSOR),
        P("section", TENSOR),
        P("section", None, None),
        P("section", None),
    )
    out_specs = (P("section", TENSOR, "dp"), P("section", TENSOR, "dp"), P("section", TENSOR, "dp"))
    return jax.shard_map(local, mesh=finer, in_specs=in_specs, out_specs=out_specs, check_vma=False)
```

profile of v0, /device:TPU:1, one launch (start us, length us, event | category | flops | bytes accessed | tf_op | source)
XLA Modules:
  0.0 455.9 jit_solution(6343559055614895578)
XLA Ops:
  8.0 0.0 copy-start
  8.0 1.3 collective-permute-start
  9.3 4.4 copy.20
  13.7 3.4 reshape_squeeze.3
  17.1 0.0 copy-done
  17.1 0.0 copy-start.9
  17.1 3.3 fusion.156
  20.4 0.0 copy-done.9
  20.4 0.6 fusion.253
  21.7 8.3 %fusion.4 = f32[384,64,52]{0,1,2:T(8,128)S(1)} fusion(f32[384,64,52]{0,2,1:T(8,128)} %fusion.156), kind=kOutput, calls=%fused_computation.7 | convolution fusion | flops 982917120 | bytes 10223616 | tf_op jit(solution)/shard_map/rac,ae->rec/dot_general | solution.py:105
  30.0 5.4 %copy.23 = f32[384,64,52]{0,2,1:T(8,128)} copy(f32[384,64,52]{0,1,2:T(8,128)S(1)} %fusion.4) | data formatting | bytes 10223616 | tf_op jit(solution)/shard_map/rac,ae->rec/transpose | solution.py:105
  35.4 0.0 copy-start.1
  35.4 6.4 %reshape.401 = f32[384,3328]{0,1:T(8,128)} reshape(f32[384,64,52]{0,2,1:T(8,128)} %copy.23) | data formatting | bytes 10223616 | tf_op jit(solution)/shard_map/reshape | solution.py:106
  41.7 0.1 fusion.207
  41.9 0.0 collective-permute-done
  41.9 0.0 copy-done.1
  41.9 0.0 copy-start.3
  41.9 0.3 multiply_reduce_fusion
  42.2 0.6 broadcast_in_dim.8
  42.8 11.6 %all-to-all-start = ((f32[16,1,384]{2,1,0:T(1,128)}), f32[16,1,384]{2,1,0:T(1,128)S(1)}, u32[]{:S(2)}, u32[]{:S(2)}) async-start(f32[16,1,384]{2,1,0:T(1,128)} %broadcast_in_dim.8), calls=%async_computation | async-start | bytes 49152 | tf_op jit(solution)/shard_map/all_to_all | solution.py:24
  54.5 4.5 fusion.3
  59.0 0.0 copy-done.3
  59.0 4.3 all-to-all-done
  63.3 0.0 copy-start.8
  63.3 0.0 copy-start.7
  63.3 0.6 copy-done.8
  63.9 4.7 %all-to-all-start.1 = ((f32[16,384,128]{1,2,0:T(8,128)}), f32[16,384,128]{1,2,0:T(8,128)S(1)}, u32[]{:S(2)}, u32[]{:S(2)}) async-start(f32[16,384,128]{1,2,0:T(8,128)} %bitcast.13), calls=%async_computation.2 | async-start | bytes 6291456 | tf_op jit(solution)/shard_map/all_to_all | solution.py:46
  68.6 0.0 all-reduce.7.cloned.1.call-start
  69.3 2.1 bitcast_select_fusion
  71.4 0.8 reduce_sum.28
  72.2 0.0 copy-done.7
  72.2 2.6 broadcast_select_fusion
  74.8 0.0 all-reduce.7.cloned.1.call-update
  74.9 0.0 all-gather.2.cloned.1.call-start
  74.9 62.6 %all-to-all-done.1 = f32[16,384,128]{1,2,0:T(8,128)S(1)} async-done(((f32[16,384,128]{1,2,0:T(8,128)}), f32[16,384,128]{1,2,0:T(8,128)S(1)}, u32[]{:S(2)}, u32[]{:S(2)}) %all-to-all-start.1) | async-done | bytes 3145760 | tf_op jit(solution)/shard_map/all_to_all | solution.py:46
  137.5 0.8 reduce_sum.29
  138.3 0.0 copy-start.5
  138.3 0.0 all-gather.2.cloned.1.call-update
  138.4 0.0 all-reduce.5.cloned.1.call-start
  138.4 15.9 %all-reduce.7.cloned.1.call-done = (bf16[384,1024]{1,0:T(8,128)(2,1)}, bf16[384,1024]{1,0:T(8,128)(2,1)}) async-done(((bf16[384,1024]{1,0:T(8,128)(2,1)}, bf16[384,1024]{1,0:T(8,128)(2,1)}), (bf16[384,1024]{1,0:T(8,128)(2,1)}, bf16[384,1024]{1,0:T(8,128)(2,1)})) %all-reduce.7.cloned.1.call-update) | async-done | bytes 1572880 | tf_op jit(solution)/shard_map/psum | solution.py:35
  154.3 0.0 all-reduce.5.cloned.1.call-update
  154.4 0.0 reduce-scatter.5.cloned.1.call-start
  154.4 56.3 %all-gather.2.cloned.1.call-done = bf16[384,2048]{0,1:T(8,128)(2,1)} async-done(((bf16[384,128]{0,1:T(8,128)(2,1)}), bf16[384,2048]{0,1:T(8,128)(2,1)}) %all-gather.2.cloned.1.call-update) | async-done | bytes 1572880 | tf_op jit(solution)/shard_map/all_gather | solution.py:115
  210.7 3.1 fusion.254
  213.8 0.0 reduce-scatter.5.cloned.1.call-update
  213.8 0.0 reduce-scatter.3.cloned.1.call-start
  213.9 41.1 %all-reduce.5.cloned.1.call-done = (bf16[384,1024]{1,0:T(8,128)(2,1)}, bf16[384,1024]{1,0:T(8,128)(2,1)}) async-done(((bf16[384,1024]{1,0:T(8,128)(2,1)}, bf16[384,1024]{1,0:T(8,128)(2,1)}), (bf16[384,1024]{1,0:T(8,128)(2,1)}, bf16[384,1024]{1,0:T(8,128)(2,1)})) %all-reduce.5.cloned.1.call-update) | async-done | bytes 1572880 | tf_op jit(solution)/shard_map/psum | solution.py:35
  255.0 0.0 copy-done.5
  255.0 0.0 copy-start.2
  255.0 0.0 copy-start.4
  255.0 0.0 copy-start.6
  255.0 2.6 convolution_bitcast_fusion
  257.6 0.0 copy-done.2
  257.6 0.0 copy-done.4
  257.7 0.0 copy-done.6
  257.7 1.4 fusion.252
  259.1 4.1 pad_maximum_fusion
  263.2 0.0 reduce-scatter.3.cloned.1.call-update
  263.2 6.4 %reduce-scatter.5.cloned.1.call-done = f32[128,256]{1,0:T(8,128)} async-done(((f32[128,2048]{1,0:T(8,128)}), f32[128,256]{1,0:T(8,128)}) %reduce-scatter.5.cloned.1.call-update) | async-done | bytes 131088 | tf_op jit(solution)/shard_map/reduce_scatter | solution.py:121
  269.6 1.6 multiply_bitcast_fusion
  271.1 174.9 %reduce-scatter.3.cloned.1.call-done = f32[2048,128]{1,0:T(8,128)} async-done(((f32[2048,1024]{1,0:T(8,128)}), f32[2048,128]{1,0:T(8,128)}) %reduce-scatter.3.cloned.1.call-update) | async-done | bytes 1048592 | tf_op jit(solution)/shard_map/reduce_scatter | solution.py:52
  446.1 2.3 fusion.8
  (1 shorter events, 0.0 us)
Async XLA Ops:
  8.0 9.1 %copy-start = (bf16[1,52,52]{2,1,0:T(8,128)(2,1)S(1)}, bf16[1,52,52]{2,1,0:T(8,128)(2,1)}, u32[]{:S(2)}) copy-start(bf16[1,52,52]{2,1,0:T(8,128)(2,1)} %param.10) | copy-start | bytes 16228
  8.0 33.8 %collective-permute-start = (bf16[384,1024]{1,0:T(8,128)(2,1)}, bf16[384,1024]{1,0:T(8,128)(2,1)S(1)}, u32[]{:S(2)}, u32[]{:S(2)}) collective-permute-start(bf16[384,1024]{1,0:T(8,128)(2,1)} %bitcast.43), channel_id=1, source_target_pairs={{0,128},{1,129},{2,130},{3,131},{4,132},{5,133},{6,134},{7,135},{8... | collective-permute-start | bytes 2359304 | tf_op jit(solution)/shard_map/ppermute | solution.py:19
  17.1 3.3 copy-start.9
  35.4 6.5 %copy-start.1 = (bf16[1,384,1024]{2,1,0:T(8,128)(2,1)S(1)}, bf16[1,384,1024]{2,1,0:T(8,128)(2,1)}, u32[]{:S(2)}) copy-start(bf16[1,384,1024]{2,1,0:T(8,128)(2,1)} %param.6) | copy-start | bytes 2359300
  41.9 17.1 %copy-start.3 = (bf16[384,1024]{1,0:T(8,128)(2,1)}, bf16[384,1024]{1,0:T(8,128)(2,1)S(1)}, u32[]{:S(2)}) copy-start(bf16[384,1024]{1,0:T(8,128)(2,1)S(1)} %collective-permute-done) | copy-start | bytes 2359300
  42.8 20.4 %all-to-all-start = ((f32[16,1,384]{2,1,0:T(1,128)}), f32[16,1,384]{2,1,0:T(1,128)S(1)}, u32[]{:S(2)}, u32[]{:S(2)}) async-start(f32[16,1,384]{2,1,0:T(1,128)} %broadcast_in_dim.8), calls=%async_computation | async-start | bytes 49152 | tf_op jit(solution)/shard_map/all_to_all | solution.py:24
  63.3 0.6 copy-start.8
  63.3 8.9 %copy-start.7 = (f32[1,1024]{1,0:T(1,128)S(1)}, f32[1,1024]{1,0:T(1,128)}, u32[]{:S(2)}) copy-start(f32[1,1024]{1,0:T(1,128)} %param.9) | copy-start | bytes 12292
  63.9 73.6 %all-to-all-start.1 = ((f32[16,384,128]{1,2,0:T(8,128)}), f32[16,384,128]{1,2,0:T(8,128)S(1)}, u32[]{:S(2)}, u32[]{:S(2)}) async-start(f32[16,384,128]{1,2,0:T(8,128)} %bitcast.13), calls=%async_computation.2 | async-start | bytes 6291456 | tf_op jit(solution)/shard_map/all_to_all | solution.py:46
  68.6 85.7 %all-reduce.7.cloned.1.call-start = ((), (), s32[]{:S(2)}) async-start(), calls=%async_computation.8 | async-start | bytes 3145728 | tf_op jit(solution)/shard_map/psum | solution.py:35
  74.9 135.8 %all-gather.2.cloned.1.call-start = ((), (), s32[]{:S(2)}) async-start(), calls=%async_computation.5 | async-start | bytes 1671168 | tf_op jit(solution)/shard_map/all_gather | solution.py:115
  138.3 116.7 %copy-start.5 = (bf16[1,384,1024]{2,1,0:T(8,128)(2,1)S(1)}, bf16[1,384,1024]{2,1,0:T(8,128)(2,1)}, u32[]{:S(2)}) copy-start(bf16[1,384,1024]{2,1,0:T(8,128)(2,1)} %param.7) | copy-start | bytes 2359300
  138.4 116.7 %all-reduce.5.cloned.1.call-start = ((), (), s32[]{:S(2)}) async-start(), calls=%async_computation.7 | async-start | bytes 3145728 | tf_op jit(solution)/shard_map/psum | solution.py:35
  154.4 115.2 %reduce-scatter.5.cloned.1.call-start = ((), (), s32[]{:S(2)}) async-start(), calls=%async_computation.6 | async-start | bytes 1179648 | tf_op jit(solution)/shard_map/reduce_scatter | solution.py:121
  213.8 232.2 %reduce-scatter.3.cloned.1.call-start = ((), (), s32[]{:S(2)}) async-start(), calls=%async_computation.4 | async-start | bytes 9437184 | tf_op jit(solution)/shard_map/reduce_scatter | solution.py:52
  255.0 2.6 copy-start.2
  255.0 2.6 copy-start.4
  255.0 2.6 copy-start.6
Sparse Core Ops, SparseCore 0:
  75.0 79.3 all-reduce.6
  157.0 97.9 all-reduce.4
Sparse Core Ops, SparseCore 1:
  138.4 72.2 all-gather.1
  213.9 55.6 reduce-scatter.4
  272.0 174.0 reduce-scatter.2
where the time goes:
time: 457 us; the launch traced here: 456 us
  waiting for transfers between devices  362 us (79%)
  local copies, waits for them, and re-layouts  21.4 us (5%)
  other arithmetic  19.1 us (4%)
  matrix products  18.8 us (4%)
  starting transfers between devices  17.8 us (4%)
  between operations  17.2 us (4%)
    reduce_scatter x1, waiting for transfers between devices, in_one_piece(): lax.psum_scatter(both, axis, scatter_dimension=dim, tiled=True)  175 us
    all_to_all x1, waiting for transfers between devices, summed_on_arrival(): lax.all_to_all(tiles, axis, split_axis=0, concat_axis=0, tiled=True)  62.6 us
    psum x2, waiting for transfers between devices, broadcast_by_axis(): x = lax.psum(x, axis)  57.1 us
    all_gather x1, waiting for transfers between devices, local(): rotated = lax.all_gather(own_cols, TENSOR, axis=1, tiled=True)  56.3 us
    all_to_all x1, starting transfers between devices, copy_for_each(): lax.all_to_all(jnp.broadcast_to(x[None], (devices, *x.shape)), axis, 0, 0...  11.6 us
  transfers between devices with their start and end apart: 8, of which 7 were waited for; matrix products, arithmetic and copies ran while one was open for 12% of the time, Pallas kernels for 0%

commit v1 on v0

--- a/solution.py
+++ b/solution.py
@@ -11,6 +11,11 @@
 BLK = 2048
 TENSOR = ("tensor_0", "tensor_1")
 EPS = 1e-05
+
+
+def all_by_exchange(array, axis, d):
+    repeated = jnp.stack([array] * lax.axis_size(axis))
+    return jnp.concatenate(lax.all_to_all(repeated, axis, 0, 0), axis=d)
 
 
 def passed_along(x, axis, by):
@@ -112,7 +117,7 @@
     signs = (1 - 2 * parity).astype(jnp.float32) / math.sqrt(order_a)
     term = window * signs[None, :]
     own_cols = summed_on_arrival(term, TENSOR, 1).astype(jnp.bfloat16)
-    rotated = lax.all_gather(own_cols, TENSOR, axis=1, tiled=True)
+    rotated = all_by_exchange(own_cols, TENSOR, 1)
     part_in = gram(normed, norm_block)
     part_o = gram(attention, attn_block)
     part_down = gram(own_cols, rotated)

time: 457 us -> 502 us (1.098)
  waiting for transfers between devices: 362 us -> 399 us
  starting transfers between devices: 17.8 us -> 27.5 us
    psum x2, waiting for transfers between devices: 57.1 us -> 160 us  [broadcast_by_axis(): x = lax.psum(x, axis)]
    all_gather x1 -> x0, waiting for transfers between devices: 56.3 us -> none  [local(): rotated = lax.all_gather(own_cols, TENSOR, axis=1, tiled=True)]
    all_to_all x0 -> x1, starting transfers between devices: none -> 9.7 us  [all_by_exchange(): return jnp.concatenate(lax.all_to_all(repeated, axis, 0, 0), axis=d)]
    reduce_scatter x1, waiting for transfers between devices: 6.36 us -> 0.03 us  [local(): lax.psum_scatter(part_down, 'dp', scatter_dimension=1, tiled=True)]
  transfers between devices with their start and end apart: 8 -> 8, of which waited for: 7 -> 5; matrix products, arithmetic and copies ran while one was open for 12% -> 10% of each run, Pallas kernels for 0% -> 0%
where the time goes in v1:
time: 502 us; the launch traced here: 501 us
  waiting for transfers between devices  399 us (79%)
  starting transfers between devices  27.5 us (5%)
  local copies, waits for them, and re-layouts  22.7 us (5%)
  matrix products  17.5 us (3%)
  other arithmetic  17.1 us (3%)
  between operations  17 us (3%)
    reduce_scatter x1, waiting for transfers between devices, in_one_piece(): lax.psum_scatter(both, axis, scatter_dimension=dim, tiled=True)  170 us
    psum x2, waiting for transfers between devices, broadcast_by_axis(): x = lax.psum(x, axis)  160 us
    all_to_all x1, waiting for transfers between devices, summed_on_arrival(): lax.all_to_all(tiles, axis, split_axis=0, concat_axis=0, tiled=True)  64.7 us
    all_to_all x1, starting transfers between devices, copy_for_each(): lax.all_to_all(jnp.broadcast_to(x[None], (devices, *x.shape)), axis, 0, 0...  11.6 us
  transfers between devices with their start and end apart: 8, of which 5 were waited for; matrix products, arithmetic and copies ran while one was open for 10% of the time, Pallas kernels for 0%

profile of v1, /device:TPU:1, one launch (start us, length us, event | category | flops | bytes accessed | tf_op | source)
XLA Modules:
  0.0 501.2 jit_solution(14144372373235077277)
XLA Ops:
  8.0 0.0 copy-start
  8.0 1.3 collective-permute-start
  9.3 4.4 copy.16
  13.7 3.4 reshape_squeeze.3
  17.1 0.0 copy-done
  17.1 0.0 copy-start.8
  17.1 3.3 fusion.156
  20.5 0.0 copy-done.8
  20.5 0.6 fusion.253
  21.7 8.3 %fusion.4 = f32[384,64,52]{0,1,2:T(8,128)S(1)} fusion(f32[384,64,52]{0,2,1:T(8,128)} %fusion.156), kind=kOutput, calls=%fused_computation.7 | convolution fusion | flops 982917120 | bytes 10223616 | tf_op jit(solution)/shard_map/rac,ae->rec/dot_general | solution.py:110
  30.0 5.4 %copy.19 = f32[384,64,52]{0,2,1:T(8,128)} copy(f32[384,64,52]{0,1,2:T(8,128)S(1)} %fusion.4) | data formatting | bytes 10223616 | tf_op jit(solution)/shard_map/rac,ae->rec/transpose | solution.py:110
  35.4 0.0 copy-start.1
  35.4 6.3 %reshape.409 = f32[384,3328]{0,1:T(8,128)} reshape(f32[384,64,52]{0,2,1:T(8,128)} %copy.19) | data formatting | bytes 10223616 | tf_op jit(solution)/shard_map/reshape | solution.py:111
  41.8 0.1 fusion.207
  41.9 0.0 collective-permute-done
  41.9 0.0 copy-done.1
  41.9 0.0 copy-start.3
  41.9 0.3 multiply_reduce_fusion
  42.2 0.6 broadcast_in_dim.8
  42.9 11.6 %all-to-all-start = ((f32[16,1,384]{2,1,0:T(1,128)}), f32[16,1,384]{2,1,0:T(1,128)S(1)}, u32[]{:S(2)}, u32[]{:S(2)}) async-start(f32[16,1,384]{2,1,0:T(1,128)} %broadcast_in_dim.8), calls=%async_computation | async-start | bytes 49152 | tf_op jit(solution)/shard_map/all_to_all | solution.py:29
  54.5 4.5 fusion.3
  59.0 0.0 copy-done.3
  59.0 4.3 all-to-all-done
  63.3 0.0 copy-start.7
  63.3 0.6 copy-done.7
  63.9 4.7 all-to-all-start.1
  69.3 2.1 bitcast_select_fusion
  71.4 0.8 reduce_sum.28
  72.2 64.7 %all-to-all-done.1 = f32[16,384,128]{1,2,0:T(8,128)S(1)} async-done(((f32[16,384,128]{1,2,0:T(8,128)}), f32[16,384,128]{1,2,0:T(8,128)S(1)}, u32[]{:S(2)}, u32[]{:S(2)}) %all-to-all-start.1) | async-done | bytes 3145760 | tf_op jit(solution)/shard_map/all_to_all | solution.py:51
  136.9 0.1 reduce_sum.29
  137.0 0.0 copy-start.2
  137.0 0.0 copy-start.4
  137.0 0.0 copy-start.6
  137.0 1.4 stack.2
  138.4 9.7 %all-to-all-start.2 = ((bf16[16,384,128]{1,2,0:T(8,128)(2,1)}), bf16[16,384,128]{1,2,0:T(8,128)(2,1)S(1)}, u32[]{:S(2)}, u32[]{:S(2)}) async-start(bf16[16,384,128]{1,2,0:T(8,128)(2,1)} %stack.2), calls=%async_computation.3 | async-start | bytes 3145728 | tf_op jit(solution)/shard_map/all_to_all | solution.py:18
  148.1 0.0 all-reduce.7.cloned.1.call-start
  148.2 0.0 copy-done.2
  148.2 0.0 copy-done.4
  148.2 0.0 copy-done.6
  148.2 1.2 broadcast_select_fusion
  149.4 0.0 all-reduce.7.cloned.1.call-update
  149.4 0.0 all-reduce.5.cloned.1.call-start
  149.5 69.4 %all-reduce.7.cloned.1.call-done = (bf16[384,1024]{1,0:T(8,128)(2,1)}, bf16[384,1024]{1,0:T(8,128)(2,1)}) async-done(((bf16[384,1024]{1,0:T(8,128)(2,1)}, bf16[384,1024]{1,0:T(8,128)(2,1)}), (bf16[384,1024]{1,0:T(8,128)(2,1)}, bf16[384,1024]{1,0:T(8,128)(2,1)})) %all-reduce.7.cloned.1.call-update) | async-done | bytes 1572880 | tf_op jit(solution)/shard_map/psum | solution.py:40
  218.8 0.0 all-reduce.5.cloned.1.call-update
  218.9 0.0 reduce-scatter.5.cloned.1.call-start
  218.9 0.0 all-to-all-done.2
  218.9 1.7 fusion.254
  220.6 0.0 reduce-scatter.5.cloned.1.call-update
  220.6 0.0 reduce-scatter.3.cloned.1.call-start
  220.7 90.6 %all-reduce.5.cloned.1.call-done = (bf16[384,1024]{1,0:T(8,128)(2,1)}, bf16[384,1024]{1,0:T(8,128)(2,1)}) async-done(((bf16[384,1024]{1,0:T(8,128)(2,1)}, bf16[384,1024]{1,0:T(8,128)(2,1)}), (bf16[384,1024]{1,0:T(8,128)(2,1)}, bf16[384,1024]{1,0:T(8,128)(2,1)})) %all-reduce.5.cloned.1.call-update) | async-done | bytes 1572880 | tf_op jit(solution)/shard_map/psum | solution.py:40
  311.3 0.0 copy-start.5
  311.3 2.7 convolution_bitcast_fusion
  314.1 0.0 copy-done.5
  314.1 1.4 fusion.252
  315.5 4.1 pad_maximum_fusion
  319.6 0.0 reduce-scatter.3.cloned.1.call-update
  319.6 0.0 reduce-scatter.5.cloned.1.call-done
  319.6 1.6 multiply_bitcast_fusion
  321.2 170.3 %reduce-scatter.3.cloned.1.call-done = f32[2048,128]{1,0:T(8,128)} async-done(((f32[2048,1024]{1,0:T(8,128)}), f32[2048,128]{1,0:T(8,128)}) %reduce-scatter.3.cloned.1.call-update) | async-done | bytes 1048592 | tf_op jit(solution)/shard_map/reduce_scatter | solution.py:57
  491.5 2.3 fusion.8
  (1 shorter events, 0.0 us)
Async XLA Ops:
  8.0 9.1 %copy-start = (bf16[1,52,52]{2,1,0:T(8,128)(2,1)S(1)}, bf16[1,52,52]{2,1,0:T(8,128)(2,1)}, u32[]{:S(2)}) copy-start(bf16[1,52,52]{2,1,0:T(8,128)(2,1)} %param.10) | copy-start | bytes 16228
  8.0 33.9 %collective-permute-start = (bf16[384,1024]{1,0:T(8,128)(2,1)}, bf16[384,1024]{1,0:T(8,128)(2,1)S(1)}, u32[]{:S(2)}, u32[]{:S(2)}) collective-permute-start(bf16[384,1024]{1,0:T(8,128)(2,1)} %bitcast.46), channel_id=1, source_target_pairs={{0,128},{1,129},{2,130},{3,131},{4,132},{5,133},{6,134},{7,135},{8... | collective-permute-start | bytes 2359304 | tf_op jit(solution)/shard_map/ppermute | solution.py:24
  17.1 3.3 copy-start.8
  35.4 6.5 %copy-start.1 = (bf16[1,384,1024]{2,1,0:T(8,128)(2,1)S(1)}, bf16[1,384,1024]{2,1,0:T(8,128)(2,1)}, u32[]{:S(2)}) copy-start(bf16[1,384,1024]{2,1,0:T(8,128)(2,1)} %param.6) | copy-start | bytes 2359300
  41.9 17.1 %copy-start.3 = (bf16[384,1024]{1,0:T(8,128)(2,1)}, bf16[384,1024]{1,0:T(8,128)(2,1)S(1)}, u32[]{:S(2)}) copy-start(bf16[384,1024]{1,0:T(8,128)(2,1)S(1)} %collective-permute-done) | copy-start | bytes 2359300
  42.9 20.4 %all-to-all-start = ((f32[16,1,384]{2,1,0:T(1,128)}), f32[16,1,384]{2,1,0:T(1,128)S(1)}, u32[]{:S(2)}, u32[]{:S(2)}) async-start(f32[16,1,384]{2,1,0:T(1,128)} %broadcast_in_dim.8), calls=%async_computation | async-start | bytes 49152 | tf_op jit(solution)/shard_map/all_to_all | solution.py:29
  63.3 0.6 copy-start.7
  63.9 72.9 %all-to-all-start.1 = ((f32[16,384,128]{1,2,0:T(8,128)}), f32[16,384,128]{1,2,0:T(8,128)S(1)}, u32[]{:S(2)}, u32[]{:S(2)}) async-start(f32[16,384,128]{1,2,0:T(8,128)} %bitcast.13), calls=%async_computation.2 | async-start | bytes 6291456 | tf_op jit(solution)/shard_map/all_to_all | solution.py:51
  137.0 11.2 %copy-start.2 = (bf16[1,384,1024]{2,1,0:T(8,128)(2,1)S(1)}, bf16[1,384,1024]{2,1,0:T(8,128)(2,1)}, u32[]{:S(2)}) copy-start(bf16[1,384,1024]{2,1,0:T(8,128)(2,1)} %param.6) | copy-start | bytes 2359300
  137.0 11.2 %copy-start.4 = (bf16[384,1024]{1,0:T(8,128)(2,1)S(1)}, bf16[384,1024]{1,0:T(8,128)(2,1)}, u32[]{:S(2)}) copy-start(bf16[384,1024]{1,0:T(8,128)(2,1)} %copy-done.3) | copy-start | bytes 2359300
  137.0 11.2 %copy-start.6 = (f32[1,1024]{1,0:T(1,128)S(1)}, f32[1,1024]{1,0:T(1,128)}, u32[]{:S(2)}) copy-start(f32[1,1024]{1,0:T(1,128)} %param.9) | copy-start | bytes 12292
  138.4 80.5 %all-to-all-start.2 = ((bf16[16,384,128]{1,2,0:T(8,128)(2,1)}), bf16[16,384,128]{1,2,0:T(8,128)(2,1)S(1)}, u32[]{:S(2)}, u32[]{:S(2)}) async-start(bf16[16,384,128]{1,2,0:T(8,128)(2,1)} %stack.2), calls=%async_computation.3 | async-start | bytes 3145728 | tf_op jit(solution)/shard_map/all_to_all | solution.py:18
  148.1 70.7 %all-reduce.7.cloned.1.call-start = ((), (), s32[]{:S(2)}) async-start(), calls=%async_computation.8 | async-start | bytes 3145728 | tf_op jit(solution)/shard_map/psum | solution.py:40
  149.4 161.9 %all-reduce.5.cloned.1.call-start = ((), (), s32[]{:S(2)}) async-start(), calls=%async_computation.7 | async-start | bytes 3145728 | tf_op jit(solution)/shard_map/psum | solution.py:40
  218.9 100.8 %reduce-scatter.5.cloned.1.call-start = ((), (), s32[]{:S(2)}) async-start(), calls=%async_computation.6 | async-start | bytes 1179648 | tf_op jit(solution)/shard_map/reduce_scatter | solution.py:126
  220.6 270.9 %reduce-scatter.3.cloned.1.call-start = ((), (), s32[]{:S(2)}) async-start(), calls=%async_computation.5 | async-start | bytes 9437184 | tf_op jit(solution)/shard_map/reduce_scatter | solution.py:57
  311.3 2.7 copy-start.5
Sparse Core Ops, SparseCore 0:
  151.3 67.4 all-reduce.6
  221.5 89.7 all-reduce.4
Sparse Core Ops, SparseCore 1:
  221.9 61.9 reduce-scatter.4
  319.7 171.8 reduce-scatter.2
